TPU v7x, 32 devices: a whole 2x2x4 slice. The times are simulated.
32 devices in a mesh: tm: 4 (over z), tmpl: 8 (over y, x, core).
Axes of the slice: x: 2, y: 2, z: 4, core: 2. Of those that a mesh axis runs over, the one named last changes fastest.
Arguments:
- strain: float32 [8, 131072], P('tmpl', 'tm'), may hold values from -6 to 6
- psd_bins: int32 [4, 65536], P(None, 'tmpl'), may hold values from 0 to 8191, as said below
- psd_values: float32 [4, 8192], P('tm'), may hold values from 0.25 to 4
- chirp_slope: int32 [16], P('tmpl'), may hold values from 0 to 1023
- chirp_curve: int32 [16], P('tmpl'), may hold values from 1 to 63
Outputs:
- snr: float32 [16, 1048576], P('tmpl', 'tm')
Inputs may be any that keep to these rules, and one draw needn't show every extreme that they name: psd_bins[r, c] names the row of psd_values that serves frequency bin r * 65536 + c.
All inputs are finite; a program needn't handle non-finite values.
Results may differ from a plain program's by a relative error of at most 0.0003.
Values sent between devices are 32-bit elements; how exact they have to be, the bound alone decides.
A program may use at most 128 MiB of HBM per device.

v0:
```python
import math
import jax
import jax.numpy as jnp
from jax import lax
from jax.sharding import PartitionSpec as P

OR = 32768
HIGHEST = lax.Precision.HIGHEST
TWO_PI = 2.0 * math.pi


def shifted(block, axis, distance):
    devices = range(lax.axis_size(axis))
    route = [(i - distance, i) for i in devices if i - distance in devices]
    return lax.ppermute(block, axis, route)


def split_sizes(length):
    count = 0
    while length > 512:
        length = length // 128
        count = count + 1
    return [length] + [128] * count


def angle_table(rows_count, cols_count, modulus, direction):
    product = (
        jnp.arange(rows_count, dtype=jnp.int32)[:, None]
        * jnp.arange(cols_count, dtype=jnp.int32)[None, :]
    )
    angles = (product % modulus).astype(jnp.float32) * (direction * TWO_PI / modulus)
    return (jnp.cos(angles), jnp.sin(angles))


def complex_left(cos_part, sin_part, real_part, imag_part):
    new_re = jnp.einsum("qp,...pk->...qk", cos_part, real_part, precision=HIGHEST) - jnp.einsum(
        "qp,...pk->...qk", sin_part, imag_part, precision=HIGHEST
    )
    new_im = jnp.einsum("qp,...pk->...qk", sin_part, real_part, precision=HIGHEST) + jnp.einsum(
        "qp,...pk->...qk", cos_part, imag_part, precision=HIGHEST
    )
    return (new_re, new_im)


def apply_sizes(real_part, imag_part, sizes, direction):
    length = real_part.shape[-1]
    if len(sizes) == 1:
        cos_part, sin_part = angle_table(length, length, length, direction)
        new_re = jnp.matmul(real_part, cos_part, precision=HIGHEST) - jnp.matmul(
            imag_part, sin_part, precision=HIGHEST
        )
        new_im = jnp.matmul(real_part, sin_part, precision=HIGHEST) + jnp.matmul(
            imag_part, cos_part, precision=HIGHEST
        )
        return (new_re, new_im)
    outer_size = sizes[0]
    inner_size = length // outer_size
    leading = real_part.shape[:-1]
    real_part = real_part.reshape(leading + (outer_size, inner_size))
    imag_part = imag_part.reshape(leading + (outer_size, inner_size))
    mat_cos, mat_sin = angle_table(outer_size, outer_size, outer_size, direction)
    real_part, imag_part = complex_left(mat_cos, mat_sin, real_part, imag_part)
    cos_part, sin_part = angle_table(outer_size, inner_size, length, direction)
    real_part, imag_part = (
        real_part * cos_part - imag_part * sin_part,
        real_part * sin_part + imag_part * cos_part,
    )
    return apply_sizes(real_part, imag_part, sizes[1:], direction)


def transform(real_part, imag_part, direction):
    length = real_part.shape[-1]
    leading = real_part.shape[:-1]
    sizes = split_sizes(length)
    new_re, new_im = apply_sizes(real_part, imag_part, sizes, direction)
    lead_count = len(leading)
    last_axis = new_re.ndim - 1
    order = tuple(range(lead_count)) + tuple(range(last_axis, lead_count - 1, -1))
    new_re = jnp.transpose(new_re, order)
    new_im = jnp.transpose(new_im, order)
    return (new_re.reshape(leading + (length,)), new_im.reshape(leading + (length,)))


def chirp_phase(frequency, slope, curve, modulus):
    high_part = frequency // 1024
    low_part = frequency % 1024
    square = 2 * high_part * low_part % (modulus // 1024) * 1024 + low_part * low_part
    square = square % modulus
    return (slope * frequency + curve * square) % modulus


def amplitude_of(frequency, k_low, k_cut):
    ratio = frequency.astype(jnp.float32) / k_low
    inside = (frequency >= k_low) & (frequency < k_cut)
    return jnp.where(inside, jnp.power(jnp.maximum(ratio, 1.0), -7.0 / 6.0), 0.0)


def template_parts(frequency, chirp_slope, chirp_curve, modulus, k_low, k_cut):
    phase = chirp_phase(frequency[None, :], chirp_slope[:, None], chirp_curve[:, None], modulus)
    angles = phase.astype(jnp.float32) * (TWO_PI / modulus)
    amplitude = amplitude_of(frequency, k_low, k_cut)
    return (amplitude * jnp.cos(angles), -amplitude * jnp.sin(angles))


def local(strain, psd_bins, psd_values, chirp_slope, chirp_curve):
    groups = lax.axis_size("tmpl")
    member = lax.axis_index("tmpl")
    own_part = strain[0]
    edge_tail = shifted(own_part, "tm", 1)
    local_seq = jnp.concatenate([edge_tail, own_part])
    sub_len = local_seq.shape[0]
    total_len = sub_len * groups
    block_len = sub_len // groups
    norm_scale = 1.0 / math.sqrt(total_len)
    k_low = total_len // 200
    k_cut = 3 * total_len // 8
    band_rows = 3 * groups // 8
    inv_psd = 1.0 / jnp.take(psd_values[0], psd_bins[:band_rows])
    local_re, local_im = transform(local_seq, jnp.zeros_like(local_seq), -1.0)
    index_k = jnp.arange(sub_len, dtype=jnp.int32)
    angles = (member * index_k % total_len).astype(jnp.float32) * (-TWO_PI / total_len)
    twist_cos = jnp.cos(angles)
    twist_sin = jnp.sin(angles)
    part_re = local_re * twist_cos - local_im * twist_sin
    part_im = local_re * twist_sin + local_im * twist_cos
    cross_cos, cross_sin = angle_table(band_rows, groups, groups, -1.0)
    piece_re = lax.all_to_all(
        part_re.reshape(groups, 1, block_len), "tmpl", split_axis=0, concat_axis=1, tiled=True
    )
    piece_im = lax.all_to_all(
        part_im.reshape(groups, 1, block_len), "tmpl", split_axis=0, concat_axis=1, tiled=True
    )
    spec_re, spec_im = complex_left(cross_cos, cross_sin, piece_re[0], piece_im[0])
    white_re = spec_re * inv_psd * norm_scale
    white_im = spec_im * inv_psd * norm_scale
    white_re, white_im, inv_whole = (
        lax.all_gather(white_re, "tmpl", axis=1, tiled=True),
        lax.all_gather(white_im, "tmpl", axis=1, tiled=True),
        lax.all_gather(inv_psd, "tmpl", axis=1, tiled=True),
    )
    band_len = band_rows * sub_len
    white_re = white_re.reshape(band_len)
    white_im = white_im.reshape(band_len)
    frequency = jnp.arange(band_len, dtype=jnp.int32)
    tmpl_re, tmpl_im = template_parts(frequency, chirp_slope, chirp_curve, total_len, k_low, k_cut)
    inv_whole = inv_whole.reshape(band_len)
    sigma_sq = jnp.sum((tmpl_re * tmpl_re + tmpl_im * tmpl_im) * inv_whole, axis=-1)
    coef_re = white_re * tmpl_re + white_im * tmpl_im
    coef_im = white_im * tmpl_re - white_re * tmpl_im
    widths = ((0, 0), (0, total_len - band_len))
    series_re, series_im = transform(jnp.pad(coef_re, widths), jnp.pad(coef_im, widths), 1.0)
    magnitude = (
        jnp.sqrt(series_re * series_re + series_im * series_im) / jnp.sqrt(sigma_sq)[..., None]
    )
    return magnitude[:, OR * groups :]


def solution(mesh):
    placed = (P("tmpl", "tm"), P(None, "tmpl"), P("tm", None), P("tmpl"), P("tmpl"))
    return jax.shard_map(
        local, mesh=mesh, in_specs=placed, out_specs=P("tmpl", "tm"), check_vma=False
    )
```

profile of v0, /device:TPU:0, one launch (start us, length us, event | category | flops | bytes accessed | tf_op | source)
XLA Modules:
  0.0 431.6 jit_solution(9449449563915326860)
XLA Ops:
  5.1 5.9 %fusion.81 = f32[512,128]{1,0:T(8,128)} fusion(), kind=kOutput, calls=%fused_computation.114 | convolution fusion | flops 406323200 | bytes 262144 | tf_op jit(solution)/shard_map/qp,...pk->...qk/dot_general | solution.py:36
  14.3 9.1 %fusion.55 = (f32[32,16384]{1,0:T(8,128)S(1)}, f32[32,16384]{1,0:T(8,128)}) fusion(), kind=kLoop, calls=%fused_computation.91 | loop fusion | flops 7340032 | bytes 4194304 | tf_op jit(solution)/shard_map/sin | solution.py:32
  23.6 135.5 %gather_fusion = f32[24576]{0:T(1024)S(1)} fusion(f32[8192]{0:T(1024)S(1)} %bitcast.120, s32[24576]{0:T(1024)S(1)} %broadcast_clamp_fusion), kind=kCustom, calls=%fused_computation | custom fusion | bytes 294912 | tf_op jit(solution)/shard_map/jit(_take)/gather | solution.py:118
  177.3 14.9 %fusion.127 = f32[128,512]{1,0:T(8,128)} fusion(f32[512,128]{1,0:T(8,128)S(1)} %convolution_add_fusion.3, f32[512,128]{1,0:T(8,128)S(1)} %convolution_subtract_fusion.3), kind=kOutput, calls=%fused_computation.182 | convolution fusion | flops 102006784 | bytes 786432 | tf_op jit(solution)/shard_map/dot_general | solution.py:49
  203.9 12.9 %all_gather.11 = f32[3,65536]{1,0:T(4,128)S(1)} all-gather(f32[3,8192]{1,0:T(4,128)S(1)} %select_divide_fusion), channel_id=1, replica_groups=mesh['tm'=4,'tmpl'=8] {'tmpl'}, dimensions={1}, use_global_device_ids=true | all-gather | bytes 884736 | tf_op jit(solution)/shard_map/all_gather | solution.py:139
  231.7 10.0 %all_gather.10 = f32[3,65536]{1,0:T(4,128)S(1)} all-gather(f32[3,8192]{1,0:T(4,128)S(1)} %fusion.3), channel_id=1, replica_groups=mesh['tm'=4,'tmpl'=8] {'tmpl'}, dimensions={1}, use_global_device_ids=true | all-gather | bytes 884736 | tf_op jit(solution)/shard_map/all_gather | solution.py:138
  246.1 11.2 %all_gather.9 = f32[3,65536]{1,0:T(4,128)S(1)} all-gather(f32[3,8192]{1,0:T(4,128)S(1)} %fusion.5), channel_id=1, replica_groups=mesh['tm'=4,'tmpl'=8] {'tmpl'}, dimensions={1}, use_global_device_ids=true | all-gather | bytes 884736 | tf_op jit(solution)/shard_map/all_gather | solution.py:137
  258.7 30.0 %multiply_subtract_fusion.1 = (f32[2,196608]{1,0:T(2,128)S(1)}, f32[2,196608]{1,0:T(2,128)S(1)}, f32[2]{0:T(128)S(1)}) fusion(f32[196608]{0:T(1024)} %mul.763, f32[196608]{0:T(1024)} %mul.743, s32[196608]{0:T(1024)} %add_select_fusion.2, s32[2]{0:T(128)S(1)} %copy-done.5, s32[2]{0:T(128)S(1)} %copy-done.6, f32[196608]{0:T(1024)} %get-tuple-element.12, ...), kind=kLoop, calls=%fused_computation.57 | loop fusion | flops 11403262 | bytes 7864344 | tf_op jit(solution)/shard_map/sub | solution.py:149
  288.7 6.9 %pad.7 = f32[2,524288]{1,0:T(2,128)S(1)} pad(f32[2,196608]{1,0:T(2,128)S(1)} %get-tuple-element.8, f32[]{:T(128)} %constant.193.clone.1), padding=0_0x0_327680 | pad | bytes 5767172 | tf_op jit(solution)/shard_map/jit(_pad)/pad | solution.py:151
  295.7 6.6 %fusion.16 = f32[2,16384,32]{1,2,0:T(8,128)S(1)} fusion(f32[1,2,32,16384]{3,1,2,0:T(2,128)S(1)} %bitcast.125), kind=kOutput, calls=%fused_computation.21 | convolution fusion | flops 402667520 | bytes 8388608 | tf_op jit(solution)/shard_map/qp,...pk->...qk/dot_general | solution.py:39
  302.3 6.8 %fusion.18 = f32[2,16384,32]{1,2,0:T(8,128)S(1)} fusion(f32[1,2,32,16384]{3,1,2,0:T(2,128)S(1)} %bitcast.126), kind=kOutput, calls=%fused_computation.23 | convolution fusion | flops 402667520 | bytes 8388608 | tf_op jit(solution)/shard_map/qp,...pk->...qk/dot_general | solution.py:36
  309.1 6.5 %pad.8 = f32[2,524288]{1,0:T(2,128)S(1)} pad(f32[2,196608]{1,0:T(2,128)S(1)} %get-tuple-element.7, f32[]{:T(128)} %constant.193.clone.1), padding=0_0x0_327680 | pad | bytes 5767172 | tf_op jit(solution)/shard_map/jit(_pad)/pad | solution.py:151
  315.6 6.7 %fusion = f32[2,32,16384]{2,1,0:T(8,128)S(1)} fusion(f32[2,16384,32]{1,2,0:T(8,128)S(1)} %fusion.18, f32[1,2,32,16384]{3,1,2,0:T(2,128)S(1)} %bitcast.121), kind=kOutput, calls=%fused_computation.3 | convolution fusion | flops 403716096 | bytes 12582912 | tf_op jit(solution)/shard_map/qp,...pk->...qk/dot_general | solution.py:36
  322.3 8.5 %multiply_subtract_fusion = (f32[2,32,16384]{2,1,0:T(8,128)}, f32[2,32,16384]{2,1,0:T(8,128)S(1)}) fusion(f32[2,32,16384]{2,1,0:T(8,128)S(1)} %fusion, f32[32,16384]{1,0:T(8,128)S(1)} %get-tuple-element.14, f32[32,16384]{1,0:T(8,128)S(1)} %copy-done.2, f32[2,16384,32]{1,2,0:T(8,128)S(1)} %fusion.16, f32[1,2,32,16384]{3,1,2,0:T(2,128)S(1)} %bitcast.122), kind=kOutput, calls=%fused_computation.33 | convolution fusion | flops 410007552 | bytes 25165824 | tf_op jit(solution)/shard_map/qp,...pk->...qk/dot_general | solution.py:39
  334.5 7.7 %fusion.8 = f32[2,32,128,128]{3,2,1,0:T(8,128)S(1)} fusion(f32[2,32,128,128]{3,2,1,0:T(8,128)S(1)} %bitcast.127), kind=kOutput, calls=%fused_computation.13 | convolution fusion | flops 1610842112 | bytes 8388608 | tf_op jit(solution)/shard_map/qp,...pk->...qk/dot_general | solution.py:36
  342.2 8.0 %fusion.6 = f32[2,32,128,128]{3,2,1,0:T(8,128)S(1)} fusion(f32[2,32,128,128]{3,2,1,0:T(8,128)S(1)} %bitcast.128), kind=kOutput, calls=%fused_computation.11 | convolution fusion | flops 1610842112 | bytes 8388608 | tf_op jit(solution)/shard_map/qp,...pk->...qk/dot_general | solution.py:39
  350.3 7.8 %fusion.26 = f32[2,32,128,128]{3,2,1,0:T(8,128)S(1)} fusion(f32[2,32,128,128]{3,2,1,0:T(8,128)S(1)} %fusion.8, f32[2,32,128,128]{3,2,1,0:T(8,128)S(1)} %bitcast.123), kind=kOutput, calls=%fused_computation.44 | convolution fusion | flops 1611890688 | bytes 12582912 | tf_op jit(solution)/shard_map/qp,...pk->...qk/dot_general | solution.py:36
  358.0 8.0 %fusion.29 = f32[2,32,128,128]{3,2,1,0:T(8,128)S(1)} fusion(f32[2,32,128,128]{3,2,1,0:T(8,128)S(1)} %fusion.6, f32[2,32,128,128]{3,2,1,0:T(8,128)S(1)} %bitcast.124), kind=kOutput, calls=%fused_computation.45 | convolution fusion | flops 1611890688 | bytes 12582912 | tf_op jit(solution)/shard_map/qp,...pk->...qk/dot_general | solution.py:39
  366.0 7.2 %fusion.48 = f32[2,32,128,128]{3,2,1,0:T(8,128)S(1)} fusion(f32[2,32,128,128]{3,2,1,0:T(8,128)S(1)} %fusion.29, f32[2,32,128,128]{3,2,1,0:T(8,128)S(1)} %fusion.26, f32[128,128]{0,1:T(8,128)S(1)} %copy.49, f32[128,128]{0,1:T(8,128)S(1)} %copy.46), kind=kOutput, calls=%fused_computation.75 | convolution fusion | flops 1613987840 | bytes 12713984 | tf_op jit(solution)/shard_map/dot_general | solution.py:52
  373.2 7.4 %fusion.46 = f32[2,32,128,128]{3,2,1,0:T(8,128)S(1)} fusion(f32[2,32,128,128]{3,2,1,0:T(8,128)S(1)} %fusion.29, f32[2,32,128,128]{3,2,1,0:T(8,128)S(1)} %fusion.26, f32[128,128]{0,1:T(8,128)S(1)} %copy.49, f32[128,128]{0,1:T(8,128)S(1)} %copy.46), kind=kOutput, calls=%fused_computation.74 | convolution fusion | flops 1613987840 | bytes 12713984 | tf_op jit(solution)/shard_map/dot_general | solution.py:49
  380.7 7.1 %fusion.50 = f32[2,32,128,128]{3,2,1,0:T(8,128)S(1)} fusion(f32[2,32,128,128]{3,2,1,0:T(8,128)S(1)} %fusion.29, f32[2,32,128,128]{3,2,1,0:T(8,128)S(1)} %fusion.26, f32[128,128]{0,1:T(8,128)S(1)} %copy.49, f32[128,128]{0,1:T(8,128)S(1)} %copy.46), kind=kOutput, calls=%fused_computation.76 | convolution fusion | flops 1613987840 | bytes 12713984 | tf_op jit(solution)/shard_map/dot_general | solution.py:49
  387.8 9.8 %sqrt_bitcast_fusion = f32[2,128,128,32]{1,2,3,0:T(8,128)} fusion(f32[2,32,128,128]{3,2,1,0:T(8,128)S(1)} %fusion.48, f32[2,32,128,128]{3,2,1,0:T(8,128)S(1)} %fusion.50, f32[2,32,128,128]{3,2,1,0:T(8,128)S(1)} %fusion.46, f32[2,32,128,128]{3,2,1,0:T(8,128)S(1)} %fusion.29, f32[2,32,128,128]{3,2,1,0:T(8,128)S(1)} %fusion.26, f32[128,128]{0,1:T(8,128)S(1)} %copy.49, ...), kind=kOutput, calls=%fused_computation.31 | convolution fusion | flops 1619230720 | bytes 25296896 | tf_op jit(solution)/shard_map/dot_general | solution.py:52
  397.6 14.8 %copy.54 = f32[2,128,128,32]{3,2,1,0:T(8,128)} copy(f32[2,128,128,32]{1,2,3,0:T(8,128)} %sqrt_bitcast_fusion) | data formatting | bytes 8388608 | tf_op jit(solution)/shard_map/sqrt | solution.py:153
  412.4 15.7 %sqrt.18 = f32[2,524288]{1,0:T(2,128)} reshape(f32[2,128,128,32]{3,2,1,0:T(8,128)} %copy.54) | data formatting | bytes 8388608 | tf_op jit(solution)/shard_map/sqrt | solution.py:153
  (57 shorter events, 65.8 us)
Async XLA Ops:
  0.0 23.5 %copy-start = (f32[1,8192]{1,0:T(1,128)S(1)}, f32[1,8192]{1,0:T(1,128)}, u32[]{:S(2)}) copy-start(f32[1,8192]{1,0:T(1,128)} %param.7) | copy-start | bytes 98308
  0.0 165.1 %collective-permute-start = (f32[32768]{0:T(1024)}, f32[32768]{0:T(1024)S(1)}, u32[]{:S(2)}, u32[]{:S(2)}) collective-permute-start(f32[32768]{0:T(1024)} %bitcast.131), channel_id=1, source_target_pairs={{0,8},{8,16},{16,24},{1,9},{9,17},{17,25},{2,10},{10,18},{18,26},{... | collective-permute-start | bytes 393224 | tf_op jit(solution)/shard_map/ppermute | solution.py:15
  11.0 12.4 %copy-start.4 = (s32[4,8192]{1,0:T(4,128)S(1)}, s32[4,8192]{1,0:T(4,128)}, u32[]{:S(2)}) copy-start(s32[4,8192]{1,0:T(4,128)} %param.6) | copy-start | bytes 393220
  159.1 6.0 %copy-start.7 = (f32[1,32768]{1,0:T(1,128)S(1)}, f32[1,32768]{1,0:T(1,128)}, u32[]{:S(2)}) copy-start(f32[1,32768]{1,0:T(1,128)} %param.5) | copy-start | bytes 393220
  175.6 16.6 %copy-start.8 = (f32[512,128]{1,0:T(8,128)}, f32[512,128]{1,0:T(8,128)S(1)}, u32[]{:S(2)}) copy-start(f32[512,128]{1,0:T(8,128)S(1)} %convolution_add_fusion.3) | copy-start | bytes 786436
  199.5 20.7 %all-to-all-start = ((f32[8,1,8192]{2,1,0:T(1,128)}), f32[8,1,8192]{2,1,0:T(1,128)}, u32[]{:S(2)}, u32[]{:S(2)}) async-start(f32[8,1,8192]{2,1,0:T(1,128)} %copy.42), calls=%async_computation | async-start | bytes 524288 | tf_op jit(solution)/shard_map/all_to_all | solution.py:127
  220.2 10.3 %all-to-all-start.1 = ((f32[8,1,8192]{2,1,0:T(1,128)}), f32[8,1,8192]{2,1,0:T(1,128)S(1)}, u32[]{:S(2)}, u32[]{:S(2)}) async-start(f32[8,1,8192]{2,1,0:T(1,128)} %copy.43), calls=%async_computation.1 | async-start | bytes 524288 | tf_op jit(solution)/shard_map/all_to_all | solution.py:130
  223.6 35.1 %copy-start.5 = (s32[2]{0:T(128)S(1)}, s32[2]{0:T(128)}, u32[]{:S(2)}) copy-start(s32[2]{0:T(128)} %param.9) | copy-start | bytes 28
  223.6 35.1 %copy-start.6 = (s32[2]{0:T(128)S(1)}, s32[2]{0:T(128)}, u32[]{:S(2)}) copy-start(s32[2]{0:T(128)} %param.8) | copy-start | bytes 28
  230.5 0.7 copy-start.3
  315.6 6.7 %copy-start.2 = (f32[32,16384]{1,0:T(8,128)S(1)}, f32[32,16384]{1,0:T(8,128)}, u32[]{:S(2)}) copy-start(f32[32,16384]{1,0:T(8,128)} %get-tuple-element.15) | copy-start | bytes 6291460
  412.4 18.8 %copy-start.1 = (f32[1,8192]{1,0:T(1,128)S(1)}, f32[1,8192]{1,0:T(1,128)}, u32[]{:S(2)}) copy-start(f32[1,8192]{1,0:T(1,128)} %param.7) | copy-start | bytes 98308
where the time goes:
time: 437 us; the launch traced here: 432 us
  local copies, waits for them, and re-layouts  192 us (44%)
  matrix products  139 us (32%)
  other arithmetic  47.9 us (11%)
  blocking collectives  34.1 us (8%)
  starting transfers between devices  12.6 us (3%)
  waiting for transfers between devices  5.36 us (1%)
    gather x2, local copies, waits for them, and re-layouts, local(): inv_psd = 1.0 / jnp.take(psd_values[0], psd_bins[:band_rows])  136 us
    sqrt x2, local copies, waits for them, and re-layouts, local(): jnp.sqrt(series_re * series_re + series_im * series_im)  30.5 us
    sub x1, other arithmetic, local(): coef_im = white_im * tmpl_re - white_re * tmpl_im  30 us
    dot_general x4, matrix products, complex_left(): jnp.einsum('qp,...pk->...qk', cos_part, imag_part, precision=HIGHEST)  22.6 us
    dot_general x2, matrix products, apply_sizes(): jnp.matmul(real_part, cos_part, precision=HIGHEST)  22 us
    dot_general x4, matrix products, complex_left(): jnp.einsum('qp,...pk->...qk', cos_part, real_part, precision=HIGHEST)  21.7 us
    dot_general x4, matrix products, complex_left(): jnp.einsum('qp,...pk->...qk', sin_part, imag_part, precision=HIGHEST)  21.7 us
    dot_general x4, matrix products, complex_left(): jnp.einsum('qp,...pk->...qk', sin_part, real_part, precision=HIGHEST)  20.8 us
  transfers between devices with their start and end apart: 3, of which 1 were waited for; matrix products, arithmetic and copies ran while one was open for 38% of the time, Pallas kernels for 0%

commit v1 on v0

--- a/solution.py
+++ b/solution.py
@@ -127,8 +127,16 @@
     piece_re = lax.all_to_all(
         part_re.reshape(groups, 1, block_len), "tmpl", split_axis=0, concat_axis=1, tiled=True
     )
-    piece_im = lax.all_to_all(
-        part_im.reshape(groups, 1, block_len), "tmpl", split_axis=0, concat_axis=1, tiled=True
+    piece_im = jnp.concatenate(
+        lax.all_to_all(
+            jnp.stack(
+                jnp.split(part_im.reshape(groups, 1, block_len), lax.axis_size("tmpl"), axis=0)
+            ),
+            "tmpl",
+            0,
+            0,
+        ),
+        axis=1,
     )
     spec_re, spec_im = complex_left(cross_cos, cross_sin, piece_re[0], piece_im[0])
     white_re = spec_re * inv_psd * norm_scale

time: 437 us -> 444 us (1.016)
    unnamed x20 -> x33, local copies, waits for them, and re-layouts: 4.42 us -> 8.86 us
  transfers between devices with their start and end apart: 3 -> 3, of which waited for: 1 -> 2; matrix products, arithmetic and copies ran while one was open for 38% -> 38% of each run, Pallas kernels for 0% -> 0%
where the time goes in v1:
time: 444 us; the launch traced here: 437 us
  local copies, waits for them, and re-layouts  196 us (44%)
  matrix products  139 us (31%)
  other arithmetic  48.9 us (11%)
  blocking collectives  32.1 us (7%)
  starting transfers between devices  12.6 us (3%)
  waiting for transfers between devices  8.87 us (2%)
    gather x2, local copies, waits for them, and re-layouts, local(): inv_psd = 1.0 / jnp.take(psd_values[0], psd_bins[:band_rows])  136 us
    sqrt x2, local copies, waits for them, and re-layouts, local(): jnp.sqrt(series_re * series_re + series_im * series_im)  30.4 us
    sub x1, other arithmetic, local(): coef_im = white_im * tmpl_re - white_re * tmpl_im  30 us
    dot_general x4, matrix products, complex_left(): jnp.einsum('qp,...pk->...qk', cos_part, imag_part, precision=HIGHEST)  22.5 us
    dot_general x4, matrix products, complex_left(): jnp.einsum('qp,...pk->...qk', cos_part, real_part, precision=HIGHEST)  21.7 us
    dot_general x4, matrix products, complex_left(): jnp.einsum('qp,...pk->...qk', sin_part, imag_part, precision=HIGHEST)  21.7 us
    dot_general x2, matrix products, apply_sizes(): jnp.matmul(real_part, cos_part, precision=HIGHEST)  21.3 us
    dot_general x4, matrix products, complex_left(): jnp.einsum('qp,...pk->...qk', sin_part, real_part, precision=HIGHEST)  20.8 us
  transfers between devices with their start and end apart: 3, of which 2 were waited for; matrix products, arithmetic and copies ran while one was open for 38% of the time, Pallas kernels for 0%

profile of v1, /device:TPU:0, one launch (start us, length us, event | category | flops | bytes accessed | tf_op | source)
XLA Modules:
  0.0 437.4 jit_solution(14373833632578255004)
XLA Ops:
  15.2 9.1 %fusion.55 = (f32[32,16384]{1,0:T(8,128)S(1)}, f32[32,16384]{1,0:T(8,128)}) fusion(), kind=kLoop, calls=%fused_computation.91 | loop fusion | flops 7340032 | bytes 4194304 | tf_op jit(solution)/shard_map/sin | solution.py:32
  24.4 135.5 %gather_fusion = f32[24576]{0:T(1024)S(1)} fusion(f32[8192]{0:T(1024)S(1)} %bitcast.132, s32[24576]{0:T(1024)S(1)} %broadcast_clamp_fusion), kind=kCustom, calls=%fused_computation | custom fusion | bytes 294912 | tf_op jit(solution)/shard_map/jit(_take)/gather | solution.py:118
  160.1 11.0 %all_gather.11 = f32[3,65536]{1,0:T(4,128)S(1)} all-gather(f32[3,8192]{1,0:T(4,128)S(1)} %select_divide_fusion), channel_id=1, replica_groups=mesh['tm'=4,'tmpl'=8] {'tmpl'}, dimensions={1}, use_global_device_ids=true | all-gather | bytes 884736 | tf_op jit(solution)/shard_map/all_gather | solution.py:147
  193.1 14.2 %fusion.131 = f32[128,512]{1,0:T(8,128)} fusion(f32[512,128]{1,0:T(8,128)S(1)} %convolution_add_fusion.3, f32[512,128]{1,0:T(8,128)S(1)} %convolution_subtract_fusion.3), kind=kOutput, calls=%fused_computation.189 | convolution fusion | flops 102006784 | bytes 786432 | tf_op jit(solution)/shard_map/dot_general | solution.py:49
  230.1 6.3 %all-to-all-done.1 = f32[8,1,1,8192]{3,2,1,0:T(1,128)S(1)} async-done(((f32[8,1,1,8192]{3,2,1,0:T(1,128)}), f32[8,1,1,8192]{3,2,1,0:T(1,128)S(1)}, u32[]{:S(2)}, u32[]{:S(2)}) %all-to-all-start.1) | async-done | bytes 262176 | tf_op jit(solution)/shard_map/all_to_all | solution.py:131
  237.6 10.0 %all_gather.10 = f32[3,65536]{1,0:T(4,128)S(1)} all-gather(f32[3,8192]{1,0:T(4,128)S(1)} %fusion.3), channel_id=1, replica_groups=mesh['tm'=4,'tmpl'=8] {'tmpl'}, dimensions={1}, use_global_device_ids=true | all-gather | bytes 884736 | tf_op jit(solution)/shard_map/all_gather | solution.py:146
  252.0 11.2 %all_gather.9 = f32[3,65536]{1,0:T(4,128)S(1)} all-gather(f32[3,8192]{1,0:T(4,128)S(1)} %fusion.5), channel_id=1, replica_groups=mesh['tm'=4,'tmpl'=8] {'tmpl'}, dimensions={1}, use_global_device_ids=true | all-gather | bytes 884736 | tf_op jit(solution)/shard_map/all_gather | solution.py:145
  264.7 30.0 %multiply_subtract_fusion.1 = (f32[2,196608]{1,0:T(2,128)S(1)}, f32[2,196608]{1,0:T(2,128)S(1)}, f32[2]{0:T(128)S(1)}) fusion(f32[196608]{0:T(1024)} %mul.753, f32[196608]{0:T(1024)} %mul.733, s32[196608]{0:T(1024)} %add_select_fusion.2, s32[2]{0:T(128)S(1)} %copy-done.6, s32[2]{0:T(128)S(1)} %copy-done.7, f32[196608]{0:T(1024)} %get-tuple-element.18, ...), kind=kLoop, calls=%fused_computation.57 | loop fusion | flops 11403262 | bytes 7864344 | tf_op jit(solution)/shard_map/sub | solution.py:157
  294.7 6.9 %pad.7 = f32[2,524288]{1,0:T(2,128)S(1)} pad(f32[2,196608]{1,0:T(2,128)S(1)} %get-tuple-element.8, f32[]{:T(128)} %constant.192.clone.1), padding=0_0x0_327680 | pad | bytes 5767172 | tf_op jit(solution)/shard_map/jit(_pad)/pad | solution.py:159
  301.6 6.6 %fusion.16 = f32[2,16384,32]{1,2,0:T(8,128)S(1)} fusion(f32[1,2,32,16384]{3,1,2,0:T(2,128)S(1)} %bitcast.137), kind=kOutput, calls=%fused_computation.21 | convolution fusion | flops 402667520 | bytes 8388608 | tf_op jit(solution)/shard_map/qp,...pk->...qk/dot_general | solution.py:39
  308.2 6.8 %fusion.18 = f32[2,16384,32]{1,2,0:T(8,128)S(1)} fusion(f32[1,2,32,16384]{3,1,2,0:T(2,128)S(1)} %bitcast.138), kind=kOutput, calls=%fused_computation.23 | convolution fusion | flops 402667520 | bytes 8388608 | tf_op jit(solution)/shard_map/qp,...pk->...qk/dot_general | solution.py:36
  315.0 6.5 %pad.8 = f32[2,524288]{1,0:T(2,128)S(1)} pad(f32[2,196608]{1,0:T(2,128)S(1)} %get-tuple-element.7, f32[]{:T(128)} %constant.192.clone.1), padding=0_0x0_327680 | pad | bytes 5767172 | tf_op jit(solution)/shard_map/jit(_pad)/pad | solution.py:159
  321.6 6.7 %fusion = f32[2,32,16384]{2,1,0:T(8,128)S(1)} fusion(f32[2,16384,32]{1,2,0:T(8,128)S(1)} %fusion.18, f32[1,2,32,16384]{3,1,2,0:T(2,128)S(1)} %bitcast.133), kind=kOutput, calls=%fused_computation.3 | convolution fusion | flops 403716096 | bytes 12582912 | tf_op jit(solution)/shard_map/qp,...pk->...qk/dot_general | solution.py:36
  328.3 8.5 %multiply_subtract_fusion = (f32[2,32,16384]{2,1,0:T(8,128)}, f32[2,32,16384]{2,1,0:T(8,128)S(1)}) fusion(f32[2,32,16384]{2,1,0:T(8,128)S(1)} %fusion, f32[32,16384]{1,0:T(8,128)S(1)} %get-tuple-element.20, f32[32,16384]{1,0:T(8,128)S(1)} %copy-done.2, f32[2,16384,32]{1,2,0:T(8,128)S(1)} %fusion.16, f32[1,2,32,16384]{3,1,2,0:T(2,128)S(1)} %bitcast.134), kind=kOutput, calls=%fused_computation.33 | convolution fusion | flops 410007552 | bytes 25165824 | tf_op jit(solution)/shard_map/qp,...pk->...qk/dot_general | solution.py:39
  340.4 7.7 %fusion.8 = f32[2,32,128,128]{3,2,1,0:T(8,128)S(1)} fusion(f32[2,32,128,128]{3,2,1,0:T(8,128)S(1)} %bitcast.139), kind=kOutput, calls=%fused_computation.13 | convolution fusion | flops 1610842112 | bytes 8388608 | tf_op jit(solution)/shard_map/qp,...pk->...qk/dot_general | solution.py:36
  348.1 8.0 %fusion.6 = f32[2,32,128,128]{3,2,1,0:T(8,128)S(1)} fusion(f32[2,32,128,128]{3,2,1,0:T(8,128)S(1)} %bitcast.140), kind=kOutput, calls=%fused_computation.11 | convolution fusion | flops 1610842112 | bytes 8388608 | tf_op jit(solution)/shard_map/qp,...pk->...qk/dot_general | solution.py:39
  356.2 7.8 %fusion.26 = f32[2,32,128,128]{3,2,1,0:T(8,128)S(1)} fusion(f32[2,32,128,128]{3,2,1,0:T(8,128)S(1)} %fusion.8, f32[2,32,128,128]{3,2,1,0:T(8,128)S(1)} %bitcast.135), kind=kOutput, calls=%fused_computation.44 | convolution fusion | flops 1611890688 | bytes 12582912 | tf_op jit(solution)/shard_map/qp,...pk->...qk/dot_general | solution.py:36
  363.9 8.0 %fusion.29 = f32[2,32,128,128]{3,2,1,0:T(8,128)S(1)} fusion(f32[2,32,128,128]{3,2,1,0:T(8,128)S(1)} %fusion.6, f32[2,32,128,128]{3,2,1,0:T(8,128)S(1)} %bitcast.136), kind=kOutput, calls=%fused_computation.45 | convolution fusion | flops 1611890688 | bytes 12582912 | tf_op jit(solution)/shard_map/qp,...pk->...qk/dot_general | solution.py:39
  371.9 7.2 %fusion.48 = f32[2,32,128,128]{3,2,1,0:T(8,128)S(1)} fusion(f32[2,32,128,128]{3,2,1,0:T(8,128)S(1)} %fusion.29, f32[2,32,128,128]{3,2,1,0:T(8,128)S(1)} %fusion.26, f32[128,128]{0,1:T(8,128)S(1)} %copy.46, f32[128,128]{0,1:T(8,128)S(1)} %copy.43), kind=kOutput, calls=%fused_computation.75 | convolution fusion | flops 1613987840 | bytes 12713984 | tf_op jit(solution)/shard_map/dot_general | solution.py:52
  379.2 7.4 %fusion.46 = f32[2,32,128,128]{3,2,1,0:T(8,128)S(1)} fusion(f32[2,32,128,128]{3,2,1,0:T(8,128)S(1)} %fusion.29, f32[2,32,128,128]{3,2,1,0:T(8,128)S(1)} %fusion.26, f32[128,128]{0,1:T(8,128)S(1)} %copy.46, f32[128,128]{0,1:T(8,128)S(1)} %copy.43), kind=kOutput, calls=%fused_computation.74 | convolution fusion | flops 1613987840 | bytes 12713984 | tf_op jit(solution)/shard_map/dot_general | solution.py:49
  386.6 7.1 %fusion.50 = f32[2,32,128,128]{3,2,1,0:T(8,128)S(1)} fusion(f32[2,32,128,128]{3,2,1,0:T(8,128)S(1)} %fusion.29, f32[2,32,128,128]{3,2,1,0:T(8,128)S(1)} %fusion.26, f32[128,128]{0,1:T(8,128)S(1)} %copy.46, f32[128,128]{0,1:T(8,128)S(1)} %copy.43), kind=kOutput, calls=%fused_computation.76 | convolution fusion | flops 1613987840 | bytes 12713984 | tf_op jit(solution)/shard_map/dot_general | solution.py:49
  393.7 9.8 %sqrt_bitcast_fusion = f32[2,128,128,32]{1,2,3,0:T(8,128)} fusion(f32[2,32,128,128]{3,2,1,0:T(8,128)S(1)} %fusion.48, f32[2,32,128,128]{3,2,1,0:T(8,128)S(1)} %fusion.50, f32[2,32,128,128]{3,2,1,0:T(8,128)S(1)} %fusion.46, f32[2,32,128,128]{3,2,1,0:T(8,128)S(1)} %fusion.29, f32[2,32,128,128]{3,2,1,0:T(8,128)S(1)} %fusion.26, f32[128,128]{0,1:T(8,128)S(1)} %copy.46, ...), kind=kOutput, calls=%fused_computation.31 | convolution fusion | flops 1619230720 | bytes 25296896 | tf_op jit(solution)/shard_map/dot_general | solution.py:52
  403.5 14.7 %copy.51 = f32[2,128,128,32]{3,2,1,0:T(8,128)} copy(f32[2,128,128,32]{1,2,3,0:T(8,128)} %sqrt_bitcast_fusion) | data formatting | bytes 8388608 | tf_op jit(solution)/shard_map/sqrt | solution.py:161
  418.2 15.7 %sqrt.18 = f32[2,524288]{1,0:T(2,128)} reshape(f32[2,128,128,32]{3,2,1,0:T(8,128)} %copy.51) | data formatting | bytes 8388608 | tf_op jit(solution)/shard_map/sqrt | solution.py:161
  (72 shorter events, 73.8 us)
Async XLA Ops:
  0.0 24.4 %copy-start = (f32[1,8192]{1,0:T(1,128)S(1)}, f32[1,8192]{1,0:T(1,128)}, u32[]{:S(2)}) copy-start(f32[1,8192]{1,0:T(1,128)} %param.7) | copy-start | bytes 98308
  0.0 180.0 %collective-permute-start = (f32[32768]{0:T(1024)}, f32[32768]{0:T(1024)}, u32[]{:S(2)}, u32[]{:S(2)}) collective-permute-start(f32[32768]{0:T(1024)} %bitcast.155), channel_id=1, source_target_pairs={{0,8},{8,16},{16,24},{1,9},{9,17},{17,25},{2,10},{10,18},{18,26},{... | collective-permute-start | bytes 393224 | tf_op jit(solution)/shard_map/ppermute | solution.py:15
  11.9 12.4 %copy-start.5 = (s32[4,8192]{1,0:T(4,128)S(1)}, s32[4,8192]{1,0:T(4,128)}, u32[]{:S(2)}) copy-start(s32[4,8192]{1,0:T(4,128)} %param.6) | copy-start | bytes 393220
  174.5 5.5 %copy-start.10 = (f32[512,128]{1,0:T(8,128)S(1)}, f32[512,128]{1,0:T(8,128)}, u32[]{:S(2)}) copy-start(f32[512,128]{1,0:T(8,128)} %fusion.81) | copy-start | bytes 786436
  174.5 11.2 %copy-start.8 = (f32[1,32768]{1,0:T(1,128)S(1)}, f32[1,32768]{1,0:T(1,128)}, u32[]{:S(2)}) copy-start(f32[1,32768]{1,0:T(1,128)} %param.5) | copy-start | bytes 393220
  191.4 15.9 %copy-start.9 = (f32[512,128]{1,0:T(8,128)}, f32[512,128]{1,0:T(8,128)S(1)}, u32[]{:S(2)}) copy-start(f32[512,128]{1,0:T(8,128)S(1)} %convolution_add_fusion.3) | copy-start | bytes 786436
  215.9 10.3 %all-to-all-start = ((f32[8,1,8192]{2,1,0:T(1,128)}), f32[8,1,8192]{2,1,0:T(1,128)S(1)}, u32[]{:S(2)}, u32[]{:S(2)}) async-start(f32[8,1,8192]{2,1,0:T(1,128)} %copy.40), calls=%async_computation | async-start | bytes 524288 | tf_op jit(solution)/shard_map/all_to_all | solution.py:127
  226.1 10.3 %copy-start.3 = (f32[8,1,8192]{2,1,0:T(1,128)}, f32[8,1,8192]{2,1,0:T(1,128)S(1)}, u32[]{:S(2)}) copy-start(f32[8,1,8192]{2,1,0:T(1,128)S(1)} %all-to-all-done) | copy-start | bytes 786436
  226.1 10.3 %all-to-all-start.1 = ((f32[8,1,1,8192]{3,2,1,0:T(1,128)}), f32[8,1,1,8192]{3,2,1,0:T(1,128)S(1)}, u32[]{:S(2)}, u32[]{:S(2)}) async-start(f32[8,1,1,8192]{3,2,1,0:T(1,128)} %constant_dynamic-update-slice_fusion), calls=%async_computation.1 | async-start | bytes 524288 | tf_op jit(solution)/shard_map/all_to_all | solution.py:131
  229.6 35.1 %copy-start.6 = (s32[2]{0:T(128)S(1)}, s32[2]{0:T(128)}, u32[]{:S(2)}) copy-start(s32[2]{0:T(128)} %param.9) | copy-start | bytes 28
  229.6 35.1 %copy-start.7 = (s32[2]{0:T(128)S(1)}, s32[2]{0:T(128)}, u32[]{:S(2)}) copy-start(s32[2]{0:T(128)} %param.8) | copy-start | bytes 28
  236.4 0.7 copy-start.4
  321.6 6.7 %copy-start.2 = (f32[32,16384]{1,0:T(8,128)S(1)}, f32[32,16384]{1,0:T(8,128)}, u32[]{:S(2)}) copy-start(f32[32,16384]{1,0:T(8,128)} %get-tuple-element.21) | copy-start | bytes 6291460
  418.2 18.8 %copy-start.1 = (f32[1,8192]{1,0:T(1,128)S(1)}, f32[1,8192]{1,0:T(1,128)}, u32[]{:S(2)}) copy-start(f32[1,8192]{1,0:T(1,128)} %param.7) | copy-start | bytes 98308
